TPU v7x, 32 devices: a whole 2x2x4 slice. The times are simulated.
32 devices in a mesh: days: 2 (over x), tm: 8 (over z, y), sta: 2 (over core).
Axes of the slice: x: 2, y: 2, z: 4, core: 2. Of those that a mesh axis runs over, the one named last changes fastest.
Arguments:
- records: bfloat16 [2048, 2048], P('sta', ('days', 'tm')), parts along dimension 1, may hold values from -6 to 6
- following: bfloat16 [2048, 510], P('sta', 'days'), parts along dimension 1, may hold values from -6 to 6
- library: bfloat16 [32, 2048, 256], P(None, ('sta', 'tm')), may hold values from -6 to 6
- template_ids: int32 [2, 8], replicated, may hold values from 0 to 31
- channel_mask: int32 [32, 2048], replicated, may hold values 0 or 1
- station_group: int32 [2048], replicated, may hold values from 0 to 127
Outputs:
- detection: float32 [2, 8, 2048], P('sta', None, ('days', 'tm')), parts along dimension 2
There are 2 independent parts, one for each index of `days`. A program takes and returns all parts, laid end to end along the dimension named above; an argument that names none is the same for every part. Nothing has to cross between parts.
All inputs are finite; a program needn't handle non-finite values.
Results may differ from a plain program's by a relative error of at most 0.0003.
Values may be sent and summed in bfloat16 or wider, within the bound.
A program may use at most 128 MiB of HBM per device.

v0:
```python
import functools

import jax
import jax.numpy as jnp
from jax import lax
from jax.experimental import pallas as pl
from jax.experimental.pallas import tpu as pltpu
from jax.sharding import PartitionSpec as P

G = 128
LANES = 128
ROWS = 16


epsilon = 1e-06


def correlate_group(chunk, window, stream_ref, temps_ref, weights_ref, out_ref, ahead, base, hankel, scale):
    length = chunk + window
    group = stream_ref.shape[0]
    start = pl.multiple_of(pl.program_id(0) * chunk, LANES)
    rows = stream_ref[:, pl.ds(start, length)]

    ahead[...] = pltpu.roll(rows, length - (ROWS - 1), 1)
    batch = min(8, group)

    def turn_rows(step, carry):
        for k in range(batch):
            s = step * batch + k
            row = jnp.broadcast_to(ahead[pl.ds(s, 1), :], (ROWS, length))
            base[s] = pltpu.roll(row, 0, 1, stride=1, stride_axis=0).astype(base.dtype)
        return carry

    lax.fori_loop(0, group // batch, turn_rows, 0)

    square = rows * rows
    high = square.astype(jnp.bfloat16)
    low = (square - high.astype(jnp.float32)).astype(jnp.bfloat16)
    depth = window + LANES
    late = lax.broadcasted_iota(jnp.int32, (depth, LANES), 0) - lax.broadcasted_iota(jnp.int32, (depth, LANES), 1)
    band = jnp.logical_and(late >= 0, late < window).astype(jnp.float32).astype(jnp.bfloat16)
    frames = [
        half[:, block * LANES : block * LANES + depth] for half in (high, low) for block in range(chunk // LANES)
    ]
    sums = jnp.dot(jnp.concatenate(frames, axis=0), band, preferred_element_type=jnp.float32)
    sums = sums[: sums.shape[0] // 2] + sums[sums.shape[0] // 2 :]
    for block in range(chunk // LANES):
        energy = sums[block * group : (block + 1) * group] / window
        scale[:, block * LANES : (block + 1) * LANES] = lax.rsqrt(energy + epsilon)

    wide = length - LANES
    slots, lanes = weights_ref.shape
    turn = lax.rem(lanes - pl.program_id(1) * group, lanes)
    weights = pltpu.roll(weights_ref[...], turn, 1)
    acc = None
    for s in range(group):
        template = [temps_ref[block, s * slots : (s + 1) * slots, :] for block in range(window // LANES)]
        squares = sum(piece * piece for piece in template)
        tmean = jnp.sum(squares, axis=1, keepdims=True) / window
        weight = weights[:, s : s + 1] * lax.rsqrt(tmean + epsilon)
        template = jnp.concatenate(template, axis=1).astype(jnp.bfloat16)
        slot = s % hankel.shape[0]
        shifted = base[s].astype(jnp.bfloat16)
        for part in range(LANES // ROWS):
            hankel[slot, part * ROWS : (part + 1) * ROWS, :] = shifted[:, part * ROWS : part * ROWS + wide]
        matrix = jnp.concatenate(
            [hankel[slot, :, step * LANES : step * LANES + chunk] for step in range(window // LANES)], axis=0
        )
        corr = jnp.dot(template, matrix, preferred_element_type=jnp.float32)
        term = corr * scale[s : s + 1, :] * weight
        acc = term if acc is None else acc + term

    parts = [acc[:, block * LANES : (block + 1) * LANES] for block in range(chunk // LANES)]

    @pl.when(pl.program_id(1) == 0)
    def _():
        for block, part in enumerate(parts):
            out_ref[block] = part

    @pl.when(pl.program_id(1) != 0)
    def _():
        for block, part in enumerate(parts):
            out_ref[block] += part


def station_sums(stream, temps, weights, out_len):
    stations = stream.shape[0]
    slots, lanes = weights.shape
    window = temps.shape[0] * LANES
    group = min(32, stations)
    chunk = min(1024, out_len)
    length = chunk + window
    full = stream.shape[1]
    groups = stations // group
    return pl.pallas_call(
        functools.partial(correlate_group, chunk, window),
        grid=(out_len // chunk, groups),
        in_specs=[
            pl.BlockSpec((group, full), lambda c, g: (g, 0)),
            pl.BlockSpec((window // LANES, group * slots, LANES), lambda c, g: (0, g, 0)),
            pl.BlockSpec((slots, lanes), lambda c, g: (0, 0)),
        ],
        out_specs=pl.BlockSpec((chunk // LANES, slots, LANES), lambda c, g: (c, 0, 0)),
        out_shape=jax.ShapeDtypeStruct((out_len // LANES, slots, LANES), jnp.float32),
        scratch_shapes=[
            pltpu.VMEM((group, length), jnp.float32),
            pltpu.VMEM((group, ROWS, length), jnp.bfloat16),
            pltpu.VMEM((2, LANES, length - LANES), jnp.bfloat16),
            pltpu.VMEM((group, chunk), jnp.float32),
        ],
        name="station_sums",
    )(stream, temps, weights)


def enter(peers):
    barrier = pltpu.get_barrier_semaphore()
    for peer in peers:
        pl.semaphore_signal(barrier, inc=1, device_id=peer, device_id_type=pl.DeviceIdType.MESH)
    pl.semaphore_wait(barrier, len(peers))


def collect_rows(
    count, ids_ref, records_ref, following_ref, library_ref, mask_ref, group_ref,
    stream_ref, temps_ref, weights_ref, held, tail, templates, own_sem, send_sem, recv_sem,
):
    me = lax.axis_index("tm")
    pull = pltpu.make_async_copy(library_ref, templates, own_sem.at[2])
    pull.start()
    rows, block_len = held.shape[1:]
    offset = pl.multiple_of(me * rows, rows)
    own = pltpu.make_async_copy(records_ref.at[pl.ds(offset, rows), :], held.at[me], own_sem.at[0])
    after = pltpu.make_async_copy(following_ref.at[pl.ds(offset, rows), :], tail, own_sem.at[1])
    own.start()
    after.start()
    others = [lax.rem(me + step, count) for step in range(1, count)]
    enter([{"tm": other} for other in others])
    copies = []
    for step, other in enumerate(others):
        copy = pltpu.make_async_remote_copy(
            src_ref=records_ref.at[pl.ds(pl.multiple_of(other * rows, rows), rows), :],
            dst_ref=held.at[me],
            send_sem=send_sem.at[step],
            recv_sem=recv_sem.at[step],
            device_id={"tm": other},
            device_id_type=pl.DeviceIdType.MESH,
        )
        copy.start()
        copies.append(copy)
    after.wait()
    out_len = count * block_len
    stream_ref[:, out_len:] = jnp.zeros((rows, stream_ref.shape[1] - out_len), jnp.float32)
    stream_ref[:, out_len : out_len + tail.shape[1]] = tail[...].astype(jnp.float32)

    stations = mask_ref.shape[1]
    slots, lanes = weights_ref.shape
    window = templates.shape[2]
    first = lax.axis_index("sta") * (rows * count) + offset
    turn = lax.rem(stations - first, stations)
    ids = [ids_ref[j // ids_ref.shape[1], j % ids_ref.shape[1]] for j in range(slots)]
    mask = jnp.concatenate([mask_ref[pl.ds(ids[j], 1), :] for j in range(slots)], axis=0)
    mask = mask.astype(jnp.float32)
    names = group_ref[...]
    onehot = lax.broadcasted_iota(jnp.int32, (G, stations), 0) == jnp.broadcast_to(names, (G, stations))
    counts = lax.dot_general(
        mask.astype(jnp.bfloat16),
        onehot.astype(jnp.float32).astype(jnp.bfloat16),
        (((1,), (1,)), ((), ())),
        preferred_element_type=jnp.float32,
    )
    mine = pltpu.roll(jnp.broadcast_to(names, (8, stations)), turn, 1)[:1, :lanes]
    chosen = lax.broadcasted_iota(jnp.int32, (G, lanes), 0) == jnp.broadcast_to(mine, (G, lanes))
    chosen = chosen.astype(jnp.float32).astype(jnp.bfloat16)
    high = jnp.floor(counts / 128.0) * 128.0
    low = counts - high
    per_station = jnp.dot(high.astype(jnp.bfloat16), chosen, preferred_element_type=jnp.float32) + jnp.dot(
        low.astype(jnp.bfloat16), chosen, preferred_element_type=jnp.float32
    )
    my_mask = pltpu.roll(mask, turn, 1)[:, :lanes]
    weights_ref[...] = my_mask * lax.rsqrt(jnp.float32(window * G) * jnp.maximum(per_station, 1.0))

    order = lax.broadcasted_iota(jnp.int32, (window, window), 1) ^ (ROWS - 1)
    turned = (lax.broadcasted_iota(jnp.int32, (window, window), 0) == order)
    turned = turned.astype(jnp.float32).astype(jnp.bfloat16)
    pull.wait()
    for j in range(slots):
        template = jnp.dot(templates[ids[j]], turned, preferred_element_type=jnp.float32)
        for block in range(window // LANES):
            temps_ref[block, pl.ds(j, rows, stride=slots), :] = template[:, block * LANES : (block + 1) * LANES]

    own.wait()
    for copy in copies:
        copy.wait()
    for block in range(count):
        stream_ref[:, block * block_len : (block + 1) * block_len] = held[block].astype(jnp.float32)


def collect_stream(template_ids, records, following, library, channel_mask, station_group, count):
    sta_rows, block_len = records.shape
    rows, window = library.shape[1:]
    slots = template_ids.size
    lanes = -(-rows // LANES) * LANES
    return pl.pallas_call(
        functools.partial(collect_rows, count),
        in_specs=[pl.BlockSpec(memory_space=pltpu.SMEM)]
        + [pl.BlockSpec(memory_space=pl.ANY)] * 3
        + [pl.BlockSpec(memory_space=pltpu.VMEM)] * 2,
        out_specs=[pl.BlockSpec(memory_space=pltpu.VMEM)] * 3,
        out_shape=[
            jax.ShapeDtypeStruct((rows, count * block_len + window), jnp.float32),
            jax.ShapeDtypeStruct((window // LANES, rows * slots, LANES), jnp.float32),
            jax.ShapeDtypeStruct((slots, lanes), jnp.float32),
        ],
        scratch_shapes=[
            pltpu.VMEM((count, rows, block_len), records.dtype),
            pltpu.VMEM((rows, following.shape[1]), following.dtype),
            pltpu.VMEM(library.shape, library.dtype),
            pltpu.SemaphoreType.DMA((3,)),
            pltpu.SemaphoreType.DMA((count - 1,)),
            pltpu.SemaphoreType.DMA((count - 1,)),
        ],
        compiler_params=pltpu.CompilerParams(collective_id=0, has_side_effects=True),
        name="collect_stream",
    )(template_ids, records, following, library, channel_mask, station_group.reshape(1, -1))


def reduce_blocks(parts_ref, out_ref, held, send_sem, recv_sem):
    blocks, halves = parts_ref.shape[0], parts_ref.shape[1]
    count = blocks * halves
    block, half = lax.axis_index("tm"), lax.axis_index("sta")
    me = block * halves + half
    others = []
    for step in range(1, count):
        other = lax.rem(me + step, count)
        others.append((other // halves, lax.rem(other, halves)))
    enter([{"tm": b, "sta": h} for b, h in others])
    copies = []
    for step, (b, h) in enumerate(others):
        copy = pltpu.make_async_remote_copy(
            src_ref=parts_ref.at[b, h],
            dst_ref=held.at[step],
            send_sem=send_sem.at[step],
            recv_sem=recv_sem.at[step],
            device_id={"tm": b, "sta": h},
            device_id_type=pl.DeviceIdType.MESH,
        )
        copy.start()
        copies.append(copy)
    total = parts_ref[block, half]
    for step, copy in enumerate(copies):
        copy.wait_recv()
        total = total + held[step]
    out_ref[...] = total
    for copy in copies:
        copy.wait_send()


def reduce_parts(parts):
    count = parts.shape[0] * parts.shape[1]
    return pl.pallas_call(
        reduce_blocks,
        in_specs=[pl.BlockSpec(memory_space=pltpu.VMEM)],
        out_specs=pl.BlockSpec(memory_space=pltpu.VMEM),
        out_shape=jax.ShapeDtypeStruct(parts.shape[2:], parts.dtype),
        scratch_shapes=[
            pltpu.VMEM((count - 1,) + parts.shape[2:], parts.dtype),
            pltpu.SemaphoreType.DMA((count - 1,)),
            pltpu.SemaphoreType.DMA((count - 1,)),
        ],
        compiler_params=pltpu.CompilerParams(collective_id=1, has_side_effects=True),
        name="reduce_parts",
    )(parts)


def shards(blocks, halves, records, following, library, template_ids, channel_mask, station_group):
    sta_rows, block_len = records.shape
    batches, per_batch = template_ids.shape
    stream, temps, weights = collect_stream(
        template_ids, records, following, library, channel_mask, station_group, blocks
    )
    sums = station_sums(stream, temps, weights, blocks * block_len)
    tiles = block_len // LANES
    parts = sums.reshape(blocks, tiles, halves, batches // halves * per_batch, LANES)
    parts = jnp.swapaxes(parts, 1, 2).reshape(blocks, halves, -1, LANES)
    mine = reduce_parts(parts).reshape(tiles, batches // halves, per_batch, LANES)
    return jnp.moveaxis(mine, 0, 2).reshape(batches // halves, per_batch, block_len)


def solution(mesh):
    placed = (
        P("sta", ("days", "tm")),
        P("sta", "days"),
        P(None, ("sta", "tm"), None),
        P(),
        P(),
        P(),
    )
    return jax.shard_map(
        functools.partial(shards, mesh.shape["tm"], mesh.shape["sta"]),
        mesh=mesh,
        in_specs=placed,
        out_specs=P("sta", None, ("days", "tm")),
        check_vma=False,
    )
```

profile of v0, /device:TPU:0, one launch (start us, length us, event | category | flops | bytes accessed | tf_op | source)
XLA Modules:
  0.0 43.6 jit_solution(12868280077016684649)
XLA Ops:
  0.0 13.6 %collect_stream.1 = (f32[128,1280]{1,0:T(8,128)}, f32[2,2048,128]{2,1,0:T(8,128)}, f32[16,128]{1,0:T(8,128)}) custom-call(s32[2,8]{1,0:T(2,128)} %ids_ref.1, bf16[1024,128]{1,0:T(8,128)(2,1)} %records_ref.1, bf16[1024,255]{1,0:T(8,128)(2,1)} %following_ref.1, bf16[32,128,256]{2,1,0:T(8,128)(2,1)} %library_ref.1, s32[32,2048]{1,0:T(8,128)} %mask_ref.1, ...), custom_call_target="tpu_custom_call" | custom-call | tf_op jit(solution)/shard_map/collect_stream/pallas_call | solution.py:202
  13.6 19.3 %station_sums.1 = f32[8,16,128]{2,1,0:T(8,128)} custom-call(f32[128,1280]{1,0:T(8,128)} %get-tuple-element.8.stream_ref, f32[2,2048,128]{2,1,0:T(8,128)} %get-tuple-element.9.temps_ref, f32[16,128]{1,0:T(8,128)} %get-tuple-element.10.weights_ref), custom_call_target="tpu_custom_call" | custom-call | tf_op jit(solution)/shard_map/station_sums/pallas_call | solution.py:95
  32.9 9.5 %reduce_parts.1 = f32[8,128]{1,0:T(8,128)} custom-call(f32[8,2,8,128]{3,2,1,0:T(8,128)} %bitcast.3), custom_call_target="tpu_custom_call" | custom-call | tf_op jit(solution)/shard_map/reduce_parts/pallas_call | solution.py:259
  42.4 1.3 %copy.8 = f32[1,8,128]{2,1,0:T(8,128)} copy(f32[1,8,128]{2,1,0:T(8,128)} %bitcast.4) | data formatting | bytes 8192
where the time goes:
time: 43.9 us; the launch traced here: 43.6 us
  Pallas kernels  42.4 us (97%)
  local copies, waits for them, and re-layouts  1.26 us (3%)
    pallas_call x1, Pallas kernels, station_sums(): pl.pallas_call(functools.partial(correlate_group, chunk, window), grid=(o...  19.3 us
    pallas_call x1, Pallas kernels, collect_stream(): pl.pallas_call(functools.partial(collect_rows, count), in_specs=[pl.Block...  13.6 us
    pallas_call x1, Pallas kernels, reduce_parts(): pl.pallas_call(reduce_blocks, in_specs=[pl.BlockSpec(memory_space=pltpu.V...  9.51 us
    unnamed x1, local copies, waits for them, and re-layouts  1.26 us

commit v1 on v0

v1 whole, which is shorter than its diff:
```python
import functools

import jax
import jax.numpy as jnp
from jax import lax
from jax.experimental import pallas as pl
from jax.experimental.pallas import tpu as pltpu
from jax.sharding import PartitionSpec as P

G = 128
LANES = 128
HOP = 8
FRAMES = LANES // HOP
PIECE = 32

epsilon = 1e-06

f32, bf16 = jnp.float32, jnp.bfloat16
NT = (((1,), (1,)), ((), ()))


def iota(shape, axis):
    return lax.broadcasted_iota(jnp.int32, shape, axis)


def as_bf16(mask):
    return mask.astype(f32).astype(bf16)


def split(x, count):
    pieces = []
    for _ in range(count):
        piece = x.astype(bf16)
        pieces.append(piece)
        x = x - piece.astype(f32)
    return pieces


def swap_blocks(tiles):
    block = iota(tiles[0].shape, 1) // FRAMES
    step = 1
    while step < len(tiles):
        odd = (block // step) % 2 == 1
        turned = list(tiles)
        for a in range(len(tiles)):
            if a & step == 0:
                low, high = tiles[a], tiles[a | step]
                turned[a] = jnp.where(odd, pltpu.roll(high, FRAMES * step, 1), low)
                turned[a | step] = jnp.where(odd, high, pltpu.roll(low, LANES - FRAMES * step, 1))
        tiles = turned
        step *= 2
    return tiles


def station_weights(ids, first, window, mask_ref, group_ref):
    stations = mask_ref.shape[1]
    turn = lax.rem(stations - first, stations)
    mask = jnp.concatenate([mask_ref[pl.ds(i, 1), :] for i in ids], axis=0).astype(f32)
    names = group_ref[...]
    onehot = iota((G, stations), 0) == jnp.broadcast_to(names, (G, stations))
    counts = lax.dot_general(mask.astype(bf16), as_bf16(onehot), NT, preferred_element_type=f32)
    mine = pltpu.roll(jnp.broadcast_to(names, (8, stations)), turn, 1)[:1, :LANES]
    chosen = as_bf16(iota((G, LANES), 0) == jnp.broadcast_to(mine, (G, LANES)))
    high = jnp.floor(counts / 128.0) * 128.0
    low = counts - high
    per_station = jnp.dot(high.astype(bf16), chosen, preferred_element_type=f32) + jnp.dot(
        low.astype(bf16), chosen, preferred_element_type=f32
    )
    my_mask = pltpu.roll(mask, turn, 1)[:, :LANES]
    return my_mask * lax.rsqrt(jnp.float32(window * G) * jnp.maximum(per_station, 1.0))


def pad_rows(x):
    if x.shape[0] == LANES:
        return x
    return jnp.concatenate([x, jnp.zeros((LANES - x.shape[0], x.shape[1]), x.dtype)], axis=0)


def prepare_templates(ids, weights, templates, temps, coef, taps, ends):
    slots, wide, rows, _ = temps.shape
    window = wide * LANES
    lane = iota((rows, LANES), 1)
    select = as_bf16(iota((16, LANES), 1) + iota((16, LANES), 0) == LANES)
    mean = jnp.zeros((rows, LANES), f32)
    for k in range(slots):
        template = templates[ids[k]]
        last = lax.dot_general(select, pad_rows(template[:, window - LANES :]), NT, preferred_element_type=f32)
        taps[pl.ds(k, HOP, stride=slots), :] = last[:HOP]
        template = template.astype(f32)
        for a in range(wide):
            temps[k, a] = template[:, a * LANES : (a + 1) * LANES]
        total = jnp.sum(template * template, axis=1, keepdims=True)
        mean = jnp.where(lane == k, total, mean)
    mean = pad_rows(mean).T[:slots]
    own = weights * lax.rsqrt(mean / window + epsilon)
    pieces = jnp.concatenate(split(own, 3), axis=0)
    repeat = as_bf16(lax.rem(iota((3 * slots, slots * LANES), 0), slots) == iota((3 * slots, slots * LANES), 1) // LANES)
    spread = lax.dot_general(pieces, repeat, (((0,), (0,)), ((), ())), preferred_element_type=f32)
    for k in range(slots):
        coef[k] = spread[:rows, k * LANES : (k + 1) * LANES]
    for g in range(rows // PIECE):
        tiles = [jnp.zeros((slots, LANES), f32)] * (HOP * PIECE // LANES)
        for d in range(1, HOP):
            place = (HOP - d) * PIECE
            part = taps[d * slots : (d + 1) * slots, :] * own
            part = pltpu.roll(part, (place - g * PIECE) % LANES, 1)
            at = place // LANES
            here = iota((slots, LANES), 1) // PIECE == (place % LANES) // PIECE
            tiles[at] = jnp.where(here, part, tiles[at])
        ends[g] = jnp.concatenate(split(jnp.concatenate(tiles, axis=1), 2), axis=0)


def build_shifts(temps, shifts):
    slots, wide, rows, _ = temps.shape
    keep = iota((HOP, LANES), 1) >= iota((HOP, LANES), 0)
    batch = min(8, rows)

    def build(step, carry):
        for b in range(batch):
            s = step * batch + b
            columns = [[] for _ in range(wide)]
            for k in range(slots):
                before = jnp.zeros((HOP, LANES), f32)
                for a in range(wide):
                    turned = pltpu.roll(temps[k, a, pl.ds(s, HOP, stride=0), :], 0, 1, stride=1, stride_axis=0)
                    columns[a].append(jnp.where(keep, turned, before))
                    before = turned
            for a in range(wide):
                shifts[s, a] = jnp.concatenate(columns[a], axis=0).astype(bf16)
        return carry

    lax.fori_loop(0, rows // batch, build, 0)


def phase_order():
    t, lane = iota((LANES, LANES), 0), iota((LANES, LANES), 1)
    return as_bf16(t == HOP * (FRAMES - 1 - lane % FRAMES) + lane // FRAMES)


def frame_at(lane):
    return lane // FRAMES * FRAMES + FRAMES - 1 - lane % FRAMES


def band_matrix(wide):
    shape = (2 * LANES, 2 * LANES)
    late = frame_at(iota(shape, 0)) - frame_at(iota(shape, 1) % LANES) - iota(shape, 1) // LANES
    return as_bf16(jnp.logical_and(late >= 0, late < wide * FRAMES))


def stretch_matrix():
    row, lane = iota((LANES, HOP * LANES), 0), iota((LANES, HOP * LANES), 1)
    same = row // FRAMES == lane // LANES
    return as_bf16(jnp.logical_and(same, lane % LANES // HOP == FRAMES - 1 - row % FRAMES))


def scales(tiles, window, order, band, level, at):
    chunk = len(tiles) - window // LANES
    wide = window // LANES
    stations = tiles[0].shape[0]
    mixed = jnp.dot(jnp.concatenate(tiles, axis=0), order, preferred_element_type=f32)
    mixed = [mixed[m * stations : (m + 1) * stations] for m in range(len(tiles))]
    main = swap_blocks(mixed[:chunk])
    lane = iota((stations, LANES), 1)
    rest = []
    for p in range(HOP):
        tail = None
        for a in range(wide):
            shift = (FRAMES * (a - p)) % LANES
            moved = pltpu.roll(mixed[chunk + a], shift, 1) if shift else mixed[chunk + a]
            tail = moved if tail is None else jnp.where(lane // FRAMES == a, moved, tail)
        rest.append(tail)
    squares = [jnp.concatenate([m * m, r * r], axis=1) for m, r in zip(main, rest)]
    pieces = [split(square, 2) for square in squares]
    sums = jnp.dot(
        jnp.concatenate([high for high, _ in pieces] + [low for _, low in pieces], axis=0),
        band[...],
        preferred_element_type=f32,
    )
    count = HOP * stations
    sums = sums[:count] + sums[count:]
    here = [sums[p * stations : (p + 1) * stations, :LANES] for p in range(HOP)]
    then = [sums[p * stations : (p + 1) * stations, LANES:] for p in range(HOP)]
    after = [None] * HOP
    for p in reversed(range(HOP)):
        after[p] = here[p] if p == HOP - 1 else here[p] + after[p + 1]
    ahead = None
    scale = []
    for j in range(HOP):
        energy = after[j] if ahead is None else after[j] + ahead
        ahead = then[j] if ahead is None else ahead + then[j]
        scale.append(lax.rsqrt(energy / window + epsilon))
        level[pl.ds(at + j, stations, stride=HOP), :] = scale[j]
    shift = LANES - wide * FRAMES
    behind = [
        jnp.where(lane < shift, pltpu.roll(main[p], shift, 1), pltpu.roll(rest[p], shift, 1)) for p in range(HOP - 1)
    ]
    return scale, behind


def end_taps(scale, behind, ends):
    slots = ends.shape[0] // 2
    stations = scale[0].shape[0]
    zero = jnp.zeros((stations, LANES), f32)
    sums = []
    for j in range(1, HOP):
        blocks = HOP if j > HOP // 2 else HOP // 2
        parts = [scale[j] * behind[j - d] if d <= j else zero for d in range(blocks, 0, -1)]
        high, low = split(jnp.concatenate(parts, axis=0), 2)
        left = ends[:, (HOP - blocks) * stations :]
        some = jnp.dot(left, high, preferred_element_type=f32)
        more = jnp.dot(left[:slots], low, preferred_element_type=f32)
        sums.append(some[:slots] + some[slots:] + more)
    return sums


def kernel(
    count, halves,
    ids_ref, records_ref, following_ref, library_ref, mask_ref, group_ref,
    out_ref,
    held, tail, templates, temps, shifts, stream, level, coef, taps, ends, order, band, stretch,
    acc, late, parts, arrived,
    own_sem, send_sem, recv_sem, out_send_sem, out_recv_sem,
):
    me, core = lax.axis_index("tm"), lax.axis_index("sta")
    slots, wide, rows, _ = temps.shape
    window = wide * LANES
    block_len = held.shape[2]
    tiles = count * block_len // LANES
    chunk = LANES // FRAMES
    offset = pl.multiple_of(me * rows, rows)

    pull = pltpu.make_async_copy(library_ref, templates, own_sem.at[0])
    own = pltpu.make_async_copy(records_ref.at[pl.ds(offset, rows), :], held.at[me], own_sem.at[1])
    after = pltpu.make_async_copy(following_ref.at[pl.ds(offset, rows), :], tail, own_sem.at[2])
    pull.start()
    own.start()
    after.start()

    others = [lax.rem(me + step, count) for step in range(1, count)]
    everyone = [(other, core) for other in others]
    everyone += [
        (lax.rem(me + step, count), lax.rem(core + turn, halves)) for turn in range(1, halves) for step in range(count)
    ]
    barrier = pltpu.get_barrier_semaphore()
    for b, h in everyone:
        pl.semaphore_signal(barrier, inc=1, device_id={"tm": b, "sta": h}, device_id_type=pl.DeviceIdType.MESH)

    ids = [ids_ref[j // ids_ref.shape[1], j % ids_ref.shape[1]] for j in range(slots)]
    first = core * (rows * count) + offset
    weights = station_weights(ids, first, window, mask_ref, group_ref)

    pl.semaphore_wait(barrier, len(everyone))

    def piece_copy(g, step, other):
        return pltpu.make_async_remote_copy(
            src_ref=records_ref.at[pl.ds(pl.multiple_of(other * rows + g * PIECE, PIECE), PIECE), :],
            dst_ref=held.at[me, pl.ds(pl.multiple_of(g * PIECE, PIECE), PIECE), :],
            send_sem=send_sem.at[g, step],
            recv_sem=recv_sem.at[g, step],
            device_id={"tm": other},
            device_id_type=pl.DeviceIdType.MESH,
        )

    for g in range(rows // PIECE):
        for step, other in enumerate(others):
            piece_copy(g, step, other).start()

    order[...] = phase_order()
    band[...] = band_matrix(wide)
    stretch[...] = stretch_matrix()
    acc[...] = jnp.zeros(acc.shape, f32)
    late[...] = jnp.zeros(late.shape, f32)
    pull.wait()
    prepare_templates(ids, weights, templates, temps, coef, taps, ends)
    build_shifts(temps, shifts)
    after.wait()
    for a in range(wide):
        width = min(LANES, tail.shape[1] - a * LANES)
        stream[tiles + a] = jnp.zeros((rows, LANES), f32)
        stream[tiles + a, :, :width] = tail[:, a * LANES : a * LANES + width].astype(f32)
    own.wait()

    inside = iota((FRAMES, LANES), 1) < LANES - HOP * (FRAMES - 1 - iota((FRAMES, LANES), 0))

    def piece(g, carry):
        for step, other in enumerate(others):
            piece_copy(g, step, other).wait()
        base = pl.multiple_of(g * PIECE, PIECE)
        span = pl.ds(base, PIECE)
        columns = []
        for m in range(tiles):
            at = m * LANES % block_len
            columns.append(held[m * LANES // block_len, span, at : at + LANES])
            stream[m, span, :] = columns[m].astype(f32)
        for a in range(wide):
            columns.append(stream[tiles + a, span, :].astype(bf16))
        for c in range(tiles // chunk):
            scale, behind = scales(
                columns[c * chunk : (c + 1) * chunk + wide], window, order[...], band, level, base * HOP
            )
            for j, part in enumerate(end_taps(scale, behind, ends[g])):
                late[c, j + 1] += part
            sums = [None] * slots
            for b in range(PIECE):
                s = base + b
                turned = [
                    pltpu.roll(stream[c * chunk + m, pl.ds(s, FRAMES, stride=0), :], HOP, 1, stride=HOP, stride_axis=0)
                    for m in range(chunk + wide)
                ]
                frames = [
                    jnp.where(inside, turned[m], turned[m + 1]).astype(bf16) for m in range(chunk + wide - 1)
                ]
                right = jnp.concatenate(
                    [jnp.concatenate(frames[a : a + chunk], axis=0) for a in range(wide)], axis=1
                )
                left = jnp.concatenate([shifts[s, a] for a in range(wide)], axis=1)
                corr = lax.dot_general(left, right, NT, preferred_element_type=f32)
                own_level = level[pl.ds(pl.multiple_of(base * HOP + b * HOP, HOP), HOP), :]
                for k in range(slots):
                    weight = own_level * coef[k, pl.ds(s, HOP, stride=0), :]
                    term = corr[k * HOP : (k + 1) * HOP] * weight
                    sums[k] = term if sums[k] is None else sums[k] + term
            for k in range(slots):
                acc[c, k * HOP : (k + 1) * HOP, :] += sums[k]
        return carry

    lax.fori_loop(0, rows // PIECE, piece, 0)

    per_half = slots // halves
    for c in range(tiles // chunk):
        for j in range(1, HOP):
            acc[c, pl.ds(j, slots, stride=HOP), :] += late[c, j]
        for h in range(halves):
            whole = [acc[c, k * HOP : (k + 1) * HOP, :] for k in range(h * per_half, (h + 1) * per_half)]
            for m, part in enumerate(swap_blocks(whole)):
                parts[c * chunk + m, h] = part

    sends = []
    per = tiles // count
    for step, (b, h) in enumerate(everyone):
        copy = pltpu.make_async_remote_copy(
            src_ref=parts.at[pl.ds(b * per, per), h],
            dst_ref=arrived.at[step],
            send_sem=out_send_sem.at[step],
            recv_sem=out_recv_sem.at[step],
            device_id={"tm": b, "sta": h},
            device_id_type=pl.DeviceIdType.MESH,
        )
        copy.start()
        sends.append(copy)
    total = parts[pl.ds(me * per, per), core]
    for step, copy in enumerate(sends):
        copy.wait_recv()
        total = total + arrived[step]
    mine = iota((HOP, LANES), 1) % HOP == iota((HOP, LANES), 0)
    for p in range(per):
        pieces = jnp.concatenate([piece.astype(f32) for piece in split(total[p], 3)], axis=0).astype(bf16)
        wider = jnp.dot(pieces, stretch[...], preferred_element_type=f32)
        wider = wider[:HOP] + wider[HOP : 2 * HOP] + wider[2 * HOP :]
        for k in range(per_half):
            line = jnp.where(mine, wider[:, k * LANES : (k + 1) * LANES], 0.0)
            out_ref[0, k : k + 1, p * LANES : (p + 1) * LANES] = jnp.sum(line, axis=0, keepdims=True)
    for copy in sends:
        copy.wait_send()


def shards(count, halves, records, following, library, template_ids, channel_mask, station_group):
    block_len = records.shape[1]
    rows, window = library.shape[1:]
    batches, per_batch = template_ids.shape
    slots = template_ids.size
    wide = window // LANES
    tiles = count * block_len // LANES
    chunks = tiles * FRAMES // LANES
    peers = count * halves - 1
    pieces = rows // PIECE
    return pl.pallas_call(
        functools.partial(kernel, count, halves),
        in_specs=[pl.BlockSpec(memory_space=pltpu.SMEM)]
        + [pl.BlockSpec(memory_space=pl.ANY)] * 3
        + [pl.BlockSpec(memory_space=pltpu.VMEM)] * 2,
        out_specs=pl.BlockSpec(memory_space=pltpu.VMEM),
        out_shape=jax.ShapeDtypeStruct((batches // halves, per_batch, block_len), f32),
        scratch_shapes=[
            pltpu.VMEM((count, rows, block_len), records.dtype),
            pltpu.VMEM((rows, following.shape[1]), following.dtype),
            pltpu.VMEM(library.shape, library.dtype),
            pltpu.VMEM((slots, wide, rows, LANES), f32),
            pltpu.VMEM((rows, wide, slots * HOP, LANES), bf16),
            pltpu.VMEM((tiles + wide, rows, LANES), f32),
            pltpu.VMEM((rows * HOP, LANES), f32),
            pltpu.VMEM((slots, rows, LANES), f32),
            pltpu.VMEM((HOP * slots, LANES), f32),
            pltpu.VMEM((pieces, 2 * slots, HOP * PIECE), bf16),
            pltpu.VMEM((LANES, LANES), bf16),
            pltpu.VMEM((2 * LANES, 2 * LANES), bf16),
            pltpu.VMEM((LANES, HOP * LANES), bf16),
            pltpu.VMEM((chunks, slots * HOP, LANES), f32),
            pltpu.VMEM((chunks, HOP, slots, LANES), f32),
            pltpu.VMEM((tiles, halves, HOP, LANES), f32),
            pltpu.VMEM((peers, tiles // count, HOP, LANES), f32),
            pltpu.SemaphoreType.DMA((3,)),
            pltpu.SemaphoreType.DMA((pieces, count - 1)),
            pltpu.SemaphoreType.DMA((pieces, count - 1)),
            pltpu.SemaphoreType.DMA((peers,)),
            pltpu.SemaphoreType.DMA((peers,)),
        ],
        compiler_params=pltpu.CompilerParams(collective_id=0, has_side_effects=True),
        name="matched_filter",
    )(template_ids, records, following, library, channel_mask, station_group.reshape(1, -1))


def solution(mesh):
    placed = (
        P("sta", ("days", "tm")),
        P("sta", "days"),
        P(None, ("sta", "tm"), None),
        P(),
        P(),
        P(),
    )
    return jax.shard_map(
        functools.partial(shards, mesh.shape["tm"], mesh.shape["sta"]),
        mesh=mesh,
        in_specs=placed,
        out_specs=P("sta", None, ("days", "tm")),
        check_vma=False,
    )
```

time: 43.9 us -> 25.7 us (0.59)
  Pallas kernels: 42.4 us -> 24.2 us
    pallas_call x3 -> x1, Pallas kernels: 42.4 us -> 24.2 us  [shards(): pl.pallas_call(functools.partial(kernel, count, halves), in_specs=[pl.Blo...]
where the time goes in v1:
time: 25.7 us; the launch traced here: 25.5 us
  Pallas kernels  24.2 us (94%)
  local copies, waits for them, and re-layouts  1.28 us (5%)
    pallas_call x1, Pallas kernels, shards(): pl.pallas_call(functools.partial(kernel, count, halves), in_specs=[pl.Blo...  24.2 us
    unnamed x1, local copies, waits for them, and re-layouts  1.28 us

profile of v1, /device:TPU:0, one launch (start us, length us, event | category | flops | bytes accessed | tf_op | source)
XLA Modules:
  0.0 25.5 jit_solution(1272616773755926160)
XLA Ops:
  0.0 24.2 %matched_filter.1 = f32[1,8,128]{2,1,0:T(8,128)} custom-call(s32[2,8]{1,0:T(2,128)} %ids_ref.1, bf16[1024,128]{1,0:T(8,128)(2,1)} %records_ref.1, bf16[1024,255]{1,0:T(8,128)(2,1)} %following_ref.1, bf16[32,128,256]{2,1,0:T(8,128)(2,1)} %library_ref.1, s32[32,2048]{1,0:T(8,128)} %mask_ref.1, s32[1,2048]{1,0:T(1,128)} %bitcast.1), custom_call_target="tpu_custom_call" | custom-call | tf_op jit(solution)/shard_map/matched_filter/pallas_call | solution.py:377
  24.2 1.3 %copy.8 = f32[1,8,128]{2,1,0:T(8,128)} copy(f32[1,8,128]{2,1,0:T(8,128)} %matched_filter.1) | data formatting | bytes 8192

commit v2 on v1

v2 whole, which is shorter than its diff:
```python
import functools

import jax
import jax.numpy as jnp
from jax import lax
from jax.experimental import pallas as pl
from jax.experimental.pallas import tpu as pltpu
from jax.sharding import PartitionSpec as P

G = 128
LANES = 128
HOP = 8
FRAMES = LANES // HOP
PAIR = 2
PIECE = 32
EARLY = 2

epsilon = 1e-06

f32, bf16 = jnp.float32, jnp.bfloat16
NT = (((1,), (1,)), ((), ()))


def iota(shape, axis):
    return lax.broadcasted_iota(jnp.int32, shape, axis)


def as_bf16(mask):
    return mask.astype(f32).astype(bf16)


def split(x, count):
    pieces = []
    for _ in range(count):
        piece = x.astype(bf16)
        pieces.append(piece)
        x = x - piece.astype(f32)
    return pieces


def swap_blocks(tiles):
    block = iota(tiles[0].shape, 1) // FRAMES
    step = 1
    while step < len(tiles):
        odd = (block // step) % 2 == 1
        turned = list(tiles)
        for a in range(len(tiles)):
            if a & step == 0:
                low, high = tiles[a], tiles[a | step]
                turned[a] = jnp.where(odd, pltpu.roll(high, FRAMES * step, 1), low)
                turned[a | step] = jnp.where(odd, high, pltpu.roll(low, LANES - FRAMES * step, 1))
        tiles = turned
        step *= 2
    return tiles


def station_weights(ids, first, window, mask_ref, group_ref):
    stations = mask_ref.shape[1]
    turn = lax.rem(stations - first, stations)
    mask = jnp.concatenate([mask_ref[pl.ds(i, 1), :] for i in ids], axis=0).astype(f32)
    names = group_ref[...]
    onehot = iota((G, stations), 0) == jnp.broadcast_to(names, (G, stations))
    counts = lax.dot_general(mask.astype(bf16), as_bf16(onehot), NT, preferred_element_type=f32)
    mine = pltpu.roll(jnp.broadcast_to(names, (8, stations)), turn, 1)[:1, :LANES]
    chosen = as_bf16(iota((G, LANES), 0) == jnp.broadcast_to(mine, (G, LANES)))
    high = jnp.floor(counts / 128.0) * 128.0
    low = counts - high
    per_station = jnp.dot(high.astype(bf16), chosen, preferred_element_type=f32) + jnp.dot(
        low.astype(bf16), chosen, preferred_element_type=f32
    )
    my_mask = pltpu.roll(mask, turn, 1)[:, :LANES]
    return my_mask * lax.rsqrt(jnp.float32(window * G) * jnp.maximum(per_station, 1.0))


def pad_rows(x):
    if x.shape[0] == LANES:
        return x
    return jnp.concatenate([x, jnp.zeros((LANES - x.shape[0], x.shape[1]), x.dtype)], axis=0)


def spread_templates(ids, templates, temps, taps):
    slots, wide, rows, _ = temps.shape
    window = wide * LANES
    lane = iota((rows, LANES), 1)
    select = as_bf16(iota((16, LANES), 1) + iota((16, LANES), 0) == LANES)
    mean = jnp.zeros((rows, LANES), f32)
    for k in range(slots):
        template = templates[ids[k]]
        last = lax.dot_general(select, pad_rows(template[:, window - LANES :]), NT, preferred_element_type=f32)
        taps[pl.ds(k, HOP, stride=slots), :] = last[:HOP]
        template = template.astype(f32)
        for a in range(wide):
            temps[k, a] = template[:, a * LANES : (a + 1) * LANES]
        total = jnp.sum(template * template, axis=1, keepdims=True)
        mean = jnp.where(lane == k, total, mean)
    return mean


def weigh_templates(weights, mean, temps, coef, taps, ends):
    slots, wide, rows, _ = temps.shape
    window = wide * LANES
    mean = pad_rows(mean).T[:slots]
    own = weights * lax.rsqrt(mean / window + epsilon)
    pieces = jnp.concatenate(split(own, 3), axis=0)
    repeat = as_bf16(lax.rem(iota((3 * slots, slots * LANES), 0), slots) == iota((3 * slots, slots * LANES), 1) // LANES)
    spread = lax.dot_general(pieces, repeat, (((0,), (0,)), ((), ())), preferred_element_type=f32)
    for k in range(slots):
        coef[k] = spread[:rows, k * LANES : (k + 1) * LANES]
    for g in range(rows // PIECE):
        tiles = [jnp.zeros((slots, LANES), f32)] * (HOP * PIECE // LANES)
        for d in range(1, HOP):
            place = (HOP - d) * PIECE
            part = taps[d * slots : (d + 1) * slots, :] * own
            part = pltpu.roll(part, (place - g * PIECE) % LANES, 1)
            at = place // LANES
            here = iota((slots, LANES), 1) // PIECE == (place % LANES) // PIECE
            tiles[at] = jnp.where(here, part, tiles[at])
        ends[g] = jnp.concatenate(split(jnp.concatenate(tiles, axis=1), 2), axis=0)


def build_shifts(temps, shifts, stations):
    slots, wide = temps.shape[:2]
    keep = iota((HOP, LANES), 1) >= iota((HOP, LANES), 0)
    for s in stations:
        columns = [[] for _ in range(wide)]
        for k in range(slots):
            before = jnp.zeros((HOP, LANES), f32)
            for a in range(wide):
                turned = pltpu.roll(temps[k, a, pl.ds(s, HOP, stride=0), :], 0, 1, stride=1, stride_axis=0)
                columns[a].append(jnp.where(keep, turned, before))
                before = turned
        for a in range(wide):
            shifts[s, a] = jnp.concatenate(columns[a], axis=0).astype(bf16)


def sample_at(lane):
    return HOP * (FRAMES - 1 - lane % FRAMES) + lane // FRAMES


def phase_order():
    return as_bf16(iota((LANES, LANES), 0) == sample_at(iota((LANES, LANES), 1)))


def band_matrix(window):
    shape = (window + 2 * LANES, 2 * LANES)
    column = iota(shape, 1)
    late = iota(shape, 0) - column // LANES * LANES - sample_at(column % LANES)
    return as_bf16(jnp.logical_and(late >= 0, late < window))


def stretch_matrix():
    row, lane = iota((LANES, HOP * LANES), 0), iota((LANES, HOP * LANES), 1)
    same = row // FRAMES == lane // LANES
    return as_bf16(jnp.logical_and(same, lane % LANES // HOP == FRAMES - 1 - row % FRAMES))


def scales(tiles, window, order, band, level, at):
    wide = window // LANES
    chunk = len(tiles) - wide
    stations = tiles[0].shape[0]
    mixed = jnp.dot(jnp.concatenate(tiles[wide:], axis=0), order, preferred_element_type=f32).astype(bf16)
    behind = swap_blocks([mixed[m * stations : (m + 1) * stations] for m in range(chunk)])
    squares = [tile.astype(f32) * tile.astype(f32) for tile in tiles]
    pieces = [split(square, 2) for square in squares]
    rows = [
        jnp.concatenate([pieces[m + a][half] for a in range(wide + 2)], axis=1)
        for half in range(2)
        for m in range(0, chunk, 2)
    ]
    sums = jnp.dot(jnp.concatenate(rows, axis=0), band[...], preferred_element_type=f32)
    count = chunk // 2 * stations
    scale = lax.rsqrt((sums[:count] + sums[count:]) / window + epsilon)
    scale = swap_blocks(
        [
            scale[m // 2 * stations : (m // 2 + 1) * stations, m % 2 * LANES : (m % 2 + 1) * LANES]
            for m in range(chunk)
        ]
    )
    for j in range(HOP):
        level[pl.ds(at + j, stations, stride=HOP), :] = scale[j]
    return scale, [part.astype(f32) for part in behind[: HOP - 1]]


def end_taps(scale, behind, ends):
    slots = ends.shape[0] // 2
    stations = scale[0].shape[0]
    zero = jnp.zeros((stations, LANES), f32)
    sums = []
    for j in range(1, HOP):
        blocks = HOP if j > HOP // 2 else HOP // 2
        parts = [scale[j] * behind[j - d] if d <= j else zero for d in range(blocks, 0, -1)]
        high, low = split(jnp.concatenate(parts, axis=0), 2)
        left = ends[:, (HOP - blocks) * stations :]
        some = jnp.dot(left, high, preferred_element_type=f32)
        more = jnp.dot(left[:slots], low, preferred_element_type=f32)
        sums.append(some[:slots] + some[slots:] + more)
    return sums


def kernel(
    count, halves,
    ids_ref, records_ref, following_ref, library_ref, mask_ref, group_ref,
    out_ref,
    ids_own, mask_own, group_own, held, tail, templates, temps, shifts, stream, level, coef, taps, ends,
    order, band, stretch, acc, late, parts, arrived,
    own_sem, meet_sem, send_sem, recv_sem, out_send_sem, out_recv_sem,
):
    me, core = lax.axis_index("tm"), lax.axis_index("sta")
    slots, wide, rows, _ = temps.shape
    window = wide * LANES
    block_len = held.shape[2]
    tiles = count * block_len // LANES
    chunk = LANES // FRAMES
    offset = pl.multiple_of(me * rows, rows)

    local = [
        pltpu.make_async_copy(ids_ref, ids_own, own_sem.at[0]),
        pltpu.make_async_copy(mask_ref, mask_own, own_sem.at[1]),
        pltpu.make_async_copy(group_ref, group_own, own_sem.at[2]),
        pltpu.make_async_copy(library_ref, templates, own_sem.at[3]),
        pltpu.make_async_copy(records_ref.at[pl.ds(offset, rows), :], held.at[me], own_sem.at[4]),
        pltpu.make_async_copy(following_ref.at[pl.ds(offset, rows), :], tail, own_sem.at[5]),
    ]
    for copy in local:
        copy.start()

    line = count // PAIR
    place, side = me // PAIR, lax.rem(me, PAIR)
    hops = [(None, me, lax.rem(core + turn, halves)) for turn in range(1, halves)]
    hops += [(None, place * PAIR + lax.rem(side + turn, PAIR), core) for turn in range(1, PAIR)]
    hops += [(place > 0, me - PAIR, core), (place < line - 1, me + PAIR, core)]
    degree = halves + PAIR - 2 + (place > 0).astype(jnp.int32) + (place < line - 1).astype(jnp.int32)

    def meeting(turn):
        return pltpu.get_barrier_semaphore() if turn == 0 else meet_sem.at[turn - 1]

    def greet(turn):
        for there, b, h in hops:
            def signal():
                pl.semaphore_signal(
                    meeting(turn), inc=1, device_id={"tm": b, "sta": h}, device_id_type=pl.DeviceIdType.MESH
                )
            if there is None:
                signal()
            else:
                pl.when(there)(signal)

    def meet(turn):
        pl.semaphore_wait(meeting(turn), degree)

    def records_copy(other, sender):
        return pltpu.make_async_remote_copy(
            src_ref=records_ref.at[pl.ds(pl.multiple_of(other * rows, rows), rows), :],
            dst_ref=held.at[sender],
            send_sem=send_sem.at[other],
            recv_sem=recv_sem.at[sender],
            device_id={"tm": other},
            device_id_type=pl.DeviceIdType.MESH,
        )

    def send(distance):
        for turn in range(PAIR):
            far = distance - (turn > 0)
            for step in sorted({far, -far}):
                if 0 <= far < line and (turn, step) != (0, 0):
                    other = (place + step) * PAIR + lax.rem(side + turn, PAIR)

                    def start(other=other):
                        records_copy(other, me).start()

                    if step == 0:
                        start()
                    else:
                        pl.when(jnp.logical_and(place + step >= 0, place + step < line))(start)

    greet(0)
    order[...] = phase_order()
    band[...] = band_matrix(window)
    stretch[...] = stretch_matrix()
    acc[...] = jnp.zeros(acc.shape, f32)
    late[...] = jnp.zeros(late.shape, f32)
    meet(0)
    greet(1)
    send(1)
    for copy in local[:3]:
        copy.wait()
    ids = [ids_own[j // ids_own.shape[1], j % ids_own.shape[1]] for j in range(slots)]
    first = core * (rows * count) + offset
    weights = station_weights(ids, first, window, mask_own, group_own)
    meet(1)
    greet(2)
    send(2)
    local[3].wait()
    mean = spread_templates(ids, templates, temps, taps)
    for turn in range(2, line + 1):
        meet(turn)
        if turn < line:
            greet(turn + 1)
            send(turn + 1)
        if turn == 2:
            weigh_templates(weights, mean, temps, coef, taps, ends)

    pieces = rows // PIECE
    stations = [range(g * PIECE, (g + 1) * PIECE) for g in range(pieces)]
    early = min(EARLY, pieces)
    for g in range(early):
        build_shifts(temps, shifts, stations[g])
    local[5].wait()
    for a in range(wide):
        width = min(LANES, tail.shape[1] - a * LANES)
        stream[tiles + a] = jnp.zeros((rows, LANES), f32)
        stream[tiles + a, :, :width] = tail[:, a * LANES : a * LANES + width].astype(f32)
    local[4].wait()
    others = [lax.rem(me + step, count) for step in range(1, count)]
    for other in others:
        records_copy(other, other).wait_recv()

    inside = iota((FRAMES, LANES), 1) < LANES - HOP * (FRAMES - 1 - iota((FRAMES, LANES), 0))
    steps = [(g, c) for g in range(pieces) for c in range(tiles // chunk)]

    def arrive(g):
        span = slice(g * PIECE, (g + 1) * PIECE)
        columns = []
        for m in range(tiles):
            at = m * LANES % block_len
            columns.append(held[m * LANES // block_len, span, at : at + LANES])
            stream[m, span, :] = columns[m].astype(f32)
        for a in range(wide):
            columns.append(stream[tiles + a, span, :].astype(bf16))
        return columns

    def measure(index, columns):
        g, c = steps[index]
        at = index % 2 * PIECE * HOP
        scale, behind = scales(columns[c * chunk : (c + 1) * chunk + wide], window, order[...], band, level, at)
        for j, part in enumerate(end_taps(scale, behind, ends[g])):
            late[c, j + 1] += part

    def correlate(index):
        g, c = steps[index]
        sums = [None] * slots
        for b, s in enumerate(stations[g]):
            turned = [
                pltpu.roll(stream[c * chunk + m, pl.ds(s, FRAMES, stride=0), :], HOP, 1, stride=HOP, stride_axis=0)
                for m in range(chunk + wide)
            ]
            frames = [jnp.where(inside, turned[m], turned[m + 1]).astype(bf16) for m in range(chunk + wide - 1)]
            right = jnp.concatenate([jnp.concatenate(frames[a : a + chunk], axis=0) for a in range(wide)], axis=1)
            left = jnp.concatenate([shifts[s, a] for a in range(wide)], axis=1)
            corr = lax.dot_general(left, right, NT, preferred_element_type=f32)
            at = (index % 2 * PIECE + b) * HOP
            own_level = level[at : at + HOP, :]
            for k in range(slots):
                weight = own_level * coef[k, pl.ds(s, HOP, stride=0), :]
                term = corr[k * HOP : (k + 1) * HOP] * weight
                sums[k] = term if sums[k] is None else sums[k] + term
        for k in range(slots):
            acc[c, k * HOP : (k + 1) * HOP, :] += sums[k]

    columns = arrive(0)
    measure(0, columns)
    for index, (g, c) in enumerate(steps):
        if index + 1 < len(steps):
            if steps[index + 1][0] != g:
                columns = arrive(g + 1)
            measure(index + 1, columns)
        if c == 0 and g + early < pieces:
            build_shifts(temps, shifts, stations[g + early])
        correlate(index)

    per_half = slots // halves
    for c in range(tiles // chunk):
        for j in range(1, HOP):
            acc[c, pl.ds(j, slots, stride=HOP), :] += late[c, j]
        for h in range(halves):
            whole = [acc[c, k * HOP : (k + 1) * HOP, :] for k in range(h * per_half, (h + 1) * per_half)]
            for m, part in enumerate(swap_blocks(whole)):
                parts[c * chunk + m, h] = part

    everyone = [(other, core) for other in others]
    everyone += [
        (lax.rem(me + step, count), lax.rem(core + turn, halves)) for turn in range(1, halves) for step in range(count)
    ]
    sends = []
    per = tiles // count
    for step, (b, h) in enumerate(everyone):
        copy = pltpu.make_async_remote_copy(
            src_ref=parts.at[pl.ds(b * per, per), h],
            dst_ref=arrived.at[step],
            send_sem=out_send_sem.at[step],
            recv_sem=out_recv_sem.at[step],
            device_id={"tm": b, "sta": h},
            device_id_type=pl.DeviceIdType.MESH,
        )
        copy.start()
        sends.append(copy)
    total = parts[pl.ds(me * per, per), core]
    for step, copy in enumerate(sends):
        copy.wait_recv()
        total = total + arrived[step]
    mine = iota((HOP, LANES), 1) % HOP == iota((HOP, LANES), 0)
    for p in range(per):
        pieces = jnp.concatenate([piece.astype(f32) for piece in split(total[p], 3)], axis=0).astype(bf16)
        wider = jnp.dot(pieces, stretch[...], preferred_element_type=f32)
        wider = wider[:HOP] + wider[HOP : 2 * HOP] + wider[2 * HOP :]
        for k in range(per_half):
            line = jnp.where(mine, wider[:, k * LANES : (k + 1) * LANES], 0.0)
            out_ref[0, k : k + 1, p * LANES : (p + 1) * LANES] = jnp.sum(line, axis=0, keepdims=True)
    for copy in sends:
        copy.wait_send()
    for other in others:
        records_copy(other, me).wait_send()


def shards(count, halves, records, following, library, template_ids, channel_mask, station_group):
    block_len = records.shape[1]
    rows, window = library.shape[1:]
    batches, per_batch = template_ids.shape
    slots = template_ids.size
    wide = window // LANES
    tiles = count * block_len // LANES
    chunks = tiles * FRAMES // LANES
    peers = count * halves - 1
    pieces = rows // PIECE
    return pl.pallas_call(
        functools.partial(kernel, count, halves),
        in_specs=[pl.BlockSpec(memory_space=pl.ANY)] * 6,
        out_specs=pl.BlockSpec(memory_space=pltpu.VMEM),
        out_shape=jax.ShapeDtypeStruct((batches // halves, per_batch, block_len), f32),
        scratch_shapes=[
            pltpu.SMEM(template_ids.shape, template_ids.dtype),
            pltpu.VMEM(channel_mask.shape, channel_mask.dtype),
            pltpu.VMEM((1, station_group.shape[0]), station_group.dtype),
            pltpu.VMEM((count, rows, block_len), records.dtype),
            pltpu.VMEM((rows, following.shape[1]), following.dtype),
            pltpu.VMEM(library.shape, library.dtype),
            pltpu.VMEM((slots, wide, rows, LANES), f32),
            pltpu.VMEM((rows, wide, slots * HOP, LANES), bf16),
            pltpu.VMEM((tiles + wide, rows, LANES), f32),
            pltpu.VMEM((2 * PIECE * HOP, LANES), f32),
            pltpu.VMEM((slots, rows, LANES), f32),
            pltpu.VMEM((HOP * slots, LANES), f32),
            pltpu.VMEM((pieces, 2 * slots, HOP * PIECE), bf16),
            pltpu.VMEM((LANES, LANES), bf16),
            pltpu.VMEM((window + 2 * LANES, 2 * LANES), bf16),
            pltpu.VMEM((LANES, HOP * LANES), bf16),
            pltpu.VMEM((chunks, slots * HOP, LANES), f32),
            pltpu.VMEM((chunks, HOP, slots, LANES), f32),
            pltpu.VMEM((tiles, halves, HOP, LANES), f32),
            pltpu.VMEM((peers, tiles // count, HOP, LANES), f32),
            pltpu.SemaphoreType.DMA((6,)),
            pltpu.SemaphoreType.REGULAR((count // PAIR,)),
            pltpu.SemaphoreType.DMA((count,)),
            pltpu.SemaphoreType.DMA((count,)),
            pltpu.SemaphoreType.DMA((peers,)),
            pltpu.SemaphoreType.DMA((peers,)),
        ],
        compiler_params=pltpu.CompilerParams(collective_id=0, has_side_effects=True),
        name="matched_filter",
    )(template_ids, records, following, library, channel_mask, station_group.reshape(1, -1))


def solution(mesh):
    placed = (
        P("sta", ("days", "tm")),
        P("sta", "days"),
        P(None, ("sta", "tm"), None),
        P(),
        P(),
        P(),
    )
    return jax.shard_map(
        functools.partial(shards, mesh.shape["tm"], mesh.shape["sta"]),
        mesh=mesh,
        in_specs=placed,
        out_specs=P("sta", None, ("days", "tm")),
        check_vma=False,
    )
```

time: 25.7 us -> 24.9 us (0.969)
  Pallas kernels: 24.2 us -> 23.4 us
    pallas_call x1, Pallas kernels: 24.2 us -> 23.4 us  [shards(): pl.pallas_call(functools.partial(kernel, count, halves), in_specs=[pl.Blo...]
where the time goes in v2:
time: 24.9 us; the launch traced here: 24.7 us
  Pallas kernels  23.4 us (94%)
  local copies, waits for them, and re-layouts  1.28 us (5%)
    pallas_call x1, Pallas kernels, shards(): pl.pallas_call(functools.partial(kernel, count, halves), in_specs=[pl.Blo...  23.4 us
    unnamed x1, local copies, waits for them, and re-layouts  1.28 us

profile of v2, /device:TPU:0, one launch (start us, length us, event | category | flops | bytes accessed | tf_op | source)
XLA Modules:
  0.0 24.7 jit_solution(10311397537278960578)
XLA Ops:
  0.0 23.4 %matched_filter.1 = f32[1,8,128]{2,1,0:T(8,128)} custom-call(s32[2,8]{1,0:T(2,128)} %ids_ref.1, bf16[1024,128]{1,0:T(8,128)(2,1)} %records_ref.1, bf16[1024,255]{1,0:T(8,128)(2,1)} %following_ref.1, bf16[32,128,256]{2,1,0:T(8,128)(2,1)} %library_ref.1, s32[32,2048]{1,0:T(8,128)} %mask_ref.1, s32[1,2048]{1,0:T(1,128)} %bitcast.1), custom_call_target="tpu_custom_call" | custom-call | tf_op jit(solution)/shard_map/matched_filter/pallas_call | solution.py:425
  23.4 1.3 %copy.8 = f32[1,8,128]{2,1,0:T(8,128)} copy(f32[1,8,128]{2,1,0:T(8,128)} %matched_filter.1) | data formatting | bytes 8192

commit v3 on v2

--- a/solution.py
+++ b/solution.py
@@ -12,8 +12,8 @@
 HOP = 8
 FRAMES = LANES // HOP
 PAIR = 2
-PIECE = 32
-EARLY = 2
+PIECE = 64
+EARLY = 1
 
 epsilon = 1e-06
 
@@ -106,14 +106,15 @@
     spread = lax.dot_general(pieces, repeat, (((0,), (0,)), ((), ())), preferred_element_type=f32)
     for k in range(slots):
         coef[k] = spread[:rows, k * LANES : (k + 1) * LANES]
-    for g in range(rows // PIECE):
-        tiles = [jnp.zeros((slots, LANES), f32)] * (HOP * PIECE // LANES)
+    piece = min(PIECE, rows)
+    for g in range(rows // piece):
+        tiles = [jnp.zeros((slots, LANES), f32)] * (HOP * piece // LANES)
         for d in range(1, HOP):
-            place = (HOP - d) * PIECE
+            place = (HOP - d) * piece
             part = taps[d * slots : (d + 1) * slots, :] * own
-            part = pltpu.roll(part, (place - g * PIECE) % LANES, 1)
+            part = pltpu.roll(part, (place - g * piece) % LANES, 1)
             at = place // LANES
-            here = iota((slots, LANES), 1) // PIECE == (place % LANES) // PIECE
+            here = iota((slots, LANES), 1) // piece == (place % LANES) // piece
             tiles[at] = jnp.where(here, part, tiles[at])
         ends[g] = jnp.concatenate(split(jnp.concatenate(tiles, axis=1), 2), axis=0)
 
@@ -300,8 +301,9 @@
         if turn == 2:
             weigh_templates(weights, mean, temps, coef, taps, ends)
 
-    pieces = rows // PIECE
-    stations = [range(g * PIECE, (g + 1) * PIECE) for g in range(pieces)]
+    piece = min(PIECE, rows)
+    pieces = rows // piece
+    stations = [range(g * piece, (g + 1) * piece) for g in range(pieces)]
     early = min(EARLY, pieces)
     for g in range(early):
         build_shifts(temps, shifts, stations[g])
@@ -319,7 +321,7 @@
     steps = [(g, c) for g in range(pieces) for c in range(tiles // chunk)]
 
     def arrive(g):
-        span = slice(g * PIECE, (g + 1) * PIECE)
+        span = slice(g * piece, (g + 1) * piece)
         columns = []
         for m in range(tiles):
             at = m * LANES % block_len
@@ -331,7 +333,7 @@
 
     def measure(index, columns):
         g, c = steps[index]
-        at = index % 2 * PIECE * HOP
+        at = index % 2 * piece * HOP
         scale, behind = scales(columns[c * chunk : (c + 1) * chunk + wide], window, order[...], band, level, at)
         for j, part in enumerate(end_taps(scale, behind, ends[g])):
             late[c, j + 1] += part
@@ -348,7 +350,7 @@
             right = jnp.concatenate([jnp.concatenate(frames[a : a + chunk], axis=0) for a in range(wide)], axis=1)
             left = jnp.concatenate([shifts[s, a] for a in range(wide)], axis=1)
             corr = lax.dot_general(left, right, NT, preferred_element_type=f32)
-            at = (index % 2 * PIECE + b) * HOP
+            at = (index % 2 * piece + b) * HOP
             own_level = level[at : at + HOP, :]
             for k in range(slots):
                 weight = own_level * coef[k, pl.ds(s, HOP, stride=0), :]
@@ -421,7 +423,8 @@
     tiles = count * block_len // LANES
     chunks = tiles * FRAMES // LANES
     peers = count * halves - 1
-    pieces = rows // PIECE
+    piece = min(PIECE, rows)
+    pieces = rows // piece
     return pl.pallas_call(
         functools.partial(kernel, count, halves),
         in_specs=[pl.BlockSpec(memory_space=pl.ANY)] * 6,
@@ -437,10 +440,10 @@
             pltpu.VMEM((slots, wide, rows, LANES), f32),
             pltpu.VMEM((rows, wide, slots * HOP, LANES), bf16),
             pltpu.VMEM((tiles + wide, rows, LANES), f32),
-            pltpu.VMEM((2 * PIECE * HOP, LANES), f32),
+            pltpu.VMEM((2 * piece * HOP, LANES), f32),
             pltpu.VMEM((slots, rows, LANES), f32),
             pltpu.VMEM((HOP * slots, LANES), f32),
-            pltpu.VMEM((pieces, 2 * slots, HOP * PIECE), bf16),
+            pltpu.VMEM((pieces, 2 * slots, HOP * piece), bf16),
             pltpu.VMEM((LANES, LANES), bf16),
             pltpu.VMEM((window + 2 * LANES, 2 * LANES), bf16),
             pltpu.VMEM((LANES, HOP * LANES), bf16),

time: 24.9 us -> 24 us (0.964)
  Pallas kernels: 23.4 us -> 22.5 us
    pallas_call x1, Pallas kernels: 23.4 us -> 22.5 us  [shards(): pl.pallas_call(functools.partial(kernel, count, halves), in_specs=[pl.Blo...]
where the time goes in v3:
time: 24 us; the launch traced here: 23.8 us
  Pallas kernels  22.5 us (94%)
  local copies, waits for them, and re-layouts  1.28 us (5%)
    pallas_call x1, Pallas kernels, shards(): pl.pallas_call(functools.partial(kernel, count, halves), in_specs=[pl.Blo...  22.5 us
    unnamed x1, local copies, waits for them, and re-layouts  1.28 us

profile of v3, /device:TPU:0, one launch (start us, length us, event | category | flops | bytes accessed | tf_op | source)
XLA Modules:
  0.0 23.8 jit_solution(16367588233459040552)
XLA Ops:
  0.0 22.5 %matched_filter.1 = f32[1,8,128]{2,1,0:T(8,128)} custom-call(s32[2,8]{1,0:T(2,128)} %ids_ref.1, bf16[1024,128]{1,0:T(8,128)(2,1)} %records_ref.1, bf16[1024,255]{1,0:T(8,128)(2,1)} %following_ref.1, bf16[32,128,256]{2,1,0:T(8,128)(2,1)} %library_ref.1, s32[32,2048]{1,0:T(8,128)} %mask_ref.1, s32[1,2048]{1,0:T(1,128)} %bitcast.1), custom_call_target="tpu_custom_call" | custom-call | tf_op jit(solution)/shard_map/matched_filter/pallas_call | solution.py:428
  22.5 1.3 %copy.8 = f32[1,8,128]{2,1,0:T(8,128)} copy(f32[1,8,128]{2,1,0:T(8,128)} %matched_filter.1) | data formatting | bytes 8192

commit v4 on v3

--- a/solution.py
+++ b/solution.py
@@ -12,7 +12,7 @@
 HOP = 8
 FRAMES = LANES // HOP
 PAIR = 2
-PIECE = 64
+PIECE = 128
 EARLY = 1
 
 epsilon = 1e-06

time: 24 us -> 23.5 us (0.979)
  Pallas kernels: 22.5 us -> 22 us
    pallas_call x1, Pallas kernels: 22.5 us -> 22 us  [shards(): pl.pallas_call(functools.partial(kernel, count, halves), in_specs=[pl.Blo...]
where the time goes in v4:
time: 23.5 us; the launch traced here: 23.3 us
  Pallas kernels  22 us (94%)
  local copies, waits for them, and re-layouts  1.28 us (5%)
    pallas_call x1, Pallas kernels, shards(): pl.pallas_call(functools.partial(kernel, count, halves), in_specs=[pl.Blo...  22 us
    unnamed x1, local copies, waits for them, and re-layouts  1.28 us

profile of v4, /device:TPU:0, one launch (start us, length us, event | category | flops | bytes accessed | tf_op | source)
XLA Modules:
  0.0 23.3 jit_solution(13934646847912695500)
XLA Ops:
  0.0 22.0 %matched_filter.1 = f32[1,8,128]{2,1,0:T(8,128)} custom-call(s32[2,8]{1,0:T(2,128)} %ids_ref.1, bf16[1024,128]{1,0:T(8,128)(2,1)} %records_ref.1, bf16[1024,255]{1,0:T(8,128)(2,1)} %following_ref.1, bf16[32,128,256]{2,1,0:T(8,128)(2,1)} %library_ref.1, s32[32,2048]{1,0:T(8,128)} %mask_ref.1, s32[1,2048]{1,0:T(1,128)} %bitcast.1), custom_call_target="tpu_custom_call" | custom-call | tf_op jit(solution)/shard_map/matched_filter/pallas_call | solution.py:428
  22.0 1.3 %copy.8 = f32[1,8,128]{2,1,0:T(8,128)} copy(f32[1,8,128]{2,1,0:T(8,128)} %matched_filter.1) | data formatting | bytes 8192
